TPU v7x, 256 devices: a whole 4x4x8 slice. The times are simulated.
256 devices in a mesh: expert: 64 (over z, y, core), replica: 4 (over x).
Axes of the slice: x: 4, y: 4, z: 8, core: 2. Of those that a mesh axis runs over, the one named last changes fastest.
Arguments:
- hidden_first: bfloat16 [2048, 4096], P(('expert', 'replica')), may hold values from -40 to 40
- hidden_second: bfloat16 [2048, 4096], P(('expert', 'replica')), may hold values from -40 to 40
- routes_first: int32 [2048, 8], P(('expert', 'replica')), may hold values from 0 to 63, all different within a row; in each aligned block of 8 rows (0 to 7, 8 to 15, ...) at most 2 rows name the same one
- routes_second: int32 [2048, 8], P(('expert', 'replica')), may hold values from 0 to 63, all different within a row; in each aligned block of 8 rows (0 to 7, 8 to 15, ...) at most 2 rows name the same one
- mixing_first: float32 [2048, 8], P(('expert', 'replica')), may hold values from 0.05 to 0.5
- mixing_second: float32 [2048, 8], P(('expert', 'replica')), may hold values from 0.05 to 0.5
- norm_gain: float32 [4096], replicated, may hold values from 0.1 to 1.9
- expert_owner: int32 [64], replicated, may hold values from 0 to 63, each once
- swap_flags: int32 [64], replicated, may hold values from 0 to 1, as said below
- gate_up_values: bfloat16 [64, 2, 4096, 1024], P('expert', None, None, 'replica'), may hold values from -0.09375 to 0.09375
- gate_up_scales: bfloat16 [64, 2, 32, 8], P('expert', None, None, 'replica'), may hold values from 0.5 to 2
- down_values: bfloat16 [64, 1024, 4096], P('expert', 'replica'), may hold values from -0.1875 to 0.1875
- down_scales: bfloat16 [64, 8, 32], P('expert', 'replica'), may hold values from 0.5 to 2
Outputs:
- output_first: bfloat16 [2048, 4096], P(('expert', 'replica'))
- output_second: bfloat16 [2048, 4096], P(('expert', 'replica'))
- gate_up_moved: bfloat16 [64, 2, 4096, 1024], P('expert', None, None, 'replica')
- gate_up_scales_moved: bfloat16 [64, 2, 32, 8], P('expert', None, None, 'replica')
- down_moved: bfloat16 [64, 1024, 4096], P('expert', 'replica')
- down_scales_moved: bfloat16 [64, 8, 32], P('expert', 'replica')
Inputs may be any that keep to these rules, and one draw needn't show every extreme that they name: swap_flags[d] equals swap_flags[(d + 32) mod 64].
All inputs are finite; a program needn't handle non-finite values.
Results may differ from a plain program's by a relative error of at most 0.012.
Values may be sent and summed in bfloat16 or wider, within the bound.
No kernel may reach another device: no remote copies, remote signals or barrier semaphores. Data moves between devices by JAX's collectives and lax.ppermute only.
A program may use at most 128 MiB of HBM per device.

v0:
```python
import jax
import jax.numpy as jnp
from jax import lax
from jax.sharding import PartitionSpec as P


def partner(block, axis, bit):
    count = lax.axis_size(axis)
    route = []
    for low in range(count):
        high = low | 1 << bit
        if high != low and high < count:
            route += [(low, high), (high, low)]
    return lax.ppermute(block, axis, route)


def dequantize(values, scales):
    height, breadth = (values.shape[-2], values.shape[-1])
    block_rows, block_cols = (scales.shape[-2], scales.shape[-1])
    leading = values.shape[:-2]
    blocked = values.astype(jnp.float32).reshape(
        leading + (block_rows, height // block_rows, block_cols, breadth // block_cols)
    )
    scaled = blocked * scales.astype(jnp.float32)[..., :, None, :, None]
    return scaled.reshape(values.shape).astype(jnp.bfloat16)


def rms_normed(hidden, norm_gain):
    widened = hidden.astype(jnp.float32)
    inverse_rms = lax.rsqrt(jnp.mean(widened * widened, axis=-1, keepdims=True) + 1e-06)
    return (widened * inverse_rms * norm_gain).astype(jnp.bfloat16)


def rounded(partial_sum):
    return lax.optimization_barrier(partial_sum.astype(jnp.bfloat16)).astype(jnp.float32)


def expert_partial(token_rows, weights):
    gate_up, down_proj = weights
    gate_act = jnp.dot(token_rows, gate_up[0], preferred_element_type=jnp.float32)
    up_act = jnp.dot(token_rows, gate_up[1], preferred_element_type=jnp.float32)
    inner_act = (jax.nn.silu(gate_act) * up_act).astype(jnp.bfloat16)
    return rounded(jnp.dot(inner_act, down_proj, preferred_element_type=jnp.float32))


def pick_slots(routes, owner_slots, experts, capacity):
    tokens_here, top_count = routes.shape
    expert_ids = jnp.arange(owner_slots.shape[0], dtype=jnp.int32)
    target = jnp.sum(jnp.where(routes[:, :, None] == expert_ids, owner_slots, 0), axis=-1).reshape(
        -1
    )
    device_ids = jnp.arange(experts, dtype=jnp.int32)
    target_hot = (target[:, None] == device_ids).astype(jnp.int32)
    earlier = jnp.cumsum(target_hot, axis=0) - target_hot
    rank_in = jnp.sum(earlier * target_hot, axis=1)
    slot_ids = target * capacity + rank_in
    columns = jnp.arange(experts * capacity, dtype=jnp.int32)
    return (
        (slot_ids[:, None] == columns)
        .astype(jnp.float32)
        .reshape(tokens_here, top_count, experts * capacity)
    )


def finish(partial_terms):
    summed = lax.psum_scatter(
        partial_terms.astype(jnp.bfloat16), "replica", scatter_dimension=0, tiled=True
    )
    return lax.all_to_all(summed, "expert", split_axis=1, concat_axis=1, tiled=True)


def decode_step(hidden, routes, mixing, norm_gain, owner_slots, weights):
    experts = lax.axis_size("expert")
    copies = lax.axis_size("replica")
    tokens_here, top_count = routes.shape
    features = hidden.shape[1]
    capacity = min(tokens_here, max(2, 2 * tokens_here * top_count // experts))
    normed = rms_normed(hidden, norm_gain)
    own_picks = pick_slots(routes, owner_slots, experts, capacity)
    pooled, pooled_routes = (
        lax.all_gather(normed, "replica", axis=0, tiled=True),
        lax.all_gather(routes, "replica", axis=0, tiled=True),
    )
    grouped = pooled_routes.reshape(copies, tokens_here, top_count)
    pick_table = jax.vmap(
        lambda route_group: pick_slots(route_group, owner_slots, experts, capacity)
    )(grouped)
    placing = jnp.sum(pick_table, axis=2).astype(jnp.bfloat16)
    outgoing = jnp.einsum(
        "rts,rtd->rsd",
        placing,
        pooled.reshape(copies, tokens_here, features),
        preferred_element_type=jnp.float32,
    )
    outgoing = outgoing.astype(jnp.bfloat16).reshape(copies, experts, capacity, features)
    arrived = lax.all_to_all(outgoing, "expert", split_axis=1, concat_axis=1, tiled=True)
    slot_count = arrived.shape[2]
    flat_rows = arrived.reshape(-1, features)
    partial_terms = expert_partial(flat_rows, weights).reshape(
        copies, experts, slot_count, features
    )
    returned = finish(partial_terms)
    mixing_matrix = jnp.einsum("tks,tk->ts", own_picks, mixing, precision=lax.Precision.HIGHEST)
    merged = jnp.dot(
        mixing_matrix,
        returned.reshape(experts * capacity, features).astype(jnp.float32),
        precision=lax.Precision.HIGHEST,
    )
    return merged.astype(jnp.bfloat16)


def body(
    hidden_first,
    hidden_second,
    routes_first,
    routes_second,
    mixing_first,
    mixing_second,
    norm_gain,
    expert_owner,
    swap_flags,
    gate_up_values,
    gate_up_scales,
    down_values,
    down_scales,
):
    experts = lax.axis_size("expert")
    halfway = experts // 2
    my_slot = lax.axis_index("expert")
    current = (gate_up_values, gate_up_scales, down_values, down_scales)
    incoming = partner(
        (gate_up_values, gate_up_scales, down_values, down_scales),
        "expert",
        experts.bit_length() - 2,
    )
    slot_ids = jnp.arange(experts, dtype=jnp.int32)
    flagged = jnp.sum(jnp.where(slot_ids == my_slot, swap_flags, 0)) == 1
    moved_arrays = tuple(
        (
            jnp.where(flagged, fresh_piece, stale_piece)
            for fresh_piece, stale_piece in zip(incoming, current)
        )
    )
    weights_before = (
        dequantize(gate_up_values[0], gate_up_scales[0]),
        dequantize(down_values[0], down_scales[0]),
    )
    output_first = decode_step(
        hidden_first, routes_first, mixing_first, norm_gain, expert_owner, weights_before
    )
    owner_flags = jnp.sum(jnp.where(expert_owner[:, None] == slot_ids, swap_flags, 0), axis=1)
    owner_after = jnp.where(owner_flags == 1, (expert_owner + halfway) % experts, expert_owner)
    weights_after = (
        dequantize(moved_arrays[0][0], moved_arrays[1][0]),
        dequantize(moved_arrays[2][0], moved_arrays[3][0]),
    )
    output_second = decode_step(
        hidden_second, routes_second, mixing_second, norm_gain, owner_after, weights_after
    )
    return (
        output_first,
        output_second,
        moved_arrays[0],
        moved_arrays[1],
        moved_arrays[2],
        moved_arrays[3],
    )


def solution(mesh):
    return jax.shard_map(
        body,
        mesh=mesh,
        in_specs=(
            P(("expert", "replica"), None),
            P(("expert", "replica"), None),
            P(("expert", "replica"), None),
            P(("expert", "replica"), None),
            P(("expert", "replica"), None),
            P(("expert", "replica"), None),
            P(),
            P(),
            P(),
            P("expert", None, None, "replica"),
            P("expert", None, None, "replica"),
            P("expert", "replica", None),
            P("expert", "replica", None),
        ),
        out_specs=(
            P(("expert", "replica"), None),
            P(("expert", "replica"), None),
            P("expert", None, None, "replica"),
            P("expert", None, None, "replica"),
            P("expert", "replica", None),
            P("expert", "replica", None),
        ),
        check_vma=False,
    )
```

profile of v0, /device:TPU:1, one launch (start us, length us, event | category | flops | bytes accessed | tf_op | source)
XLA Modules:
  0.0 738.2 jit_solution(4624766096503249148)
XLA Ops:
  8.7 10.4 %all_gather.14 = s32[32,8]{1,0:T(8,128)S(1)} all-gather(s32[8,8]{1,0:T(8,128)} %param.16), channel_id=1, replica_groups=mesh['expert'=64,'replica'=4] {'replica'}, dimensions={0}, use_global_device_ids=true | all-gather | bytes 1280 | tf_op jit(solution)/shard_map/all_gather | solution.py:82
  23.6 9.4 %all_gather.15 = bf16[32,4096]{1,0:T(8,128)(2,1)S(1)} all-gather(bf16[8,4096]{1,0:T(8,128)(2,1)S(1)} %get-tuple-element.13), channel_id=1, replica_groups=mesh['expert'=64,'replica'=4] {'replica'}, dimensions={0}, use_global_device_ids=true | all-gather | bytes 327680 | tf_op jit(solution)/shard_map/all_gather | solution.py:81
  36.3 7.6 %reshape.189 = bf16[4,64,2,4096]{3,2,1,0:T(2,128)(2,1)} reshape(bf16[4,128,4096]{2,1,0:T(8,128)(2,1)} %convolution_convert_fusion.1) | data formatting | bytes 8388608 | tf_op jit(solution)/shard_map/reshape | solution.py:95
  43.9 10.2 %copy.44 = bf16[4,64,2,4096]{3,2,0,1:T(2,128)(2,1)} copy(bf16[4,64,2,4096]{3,2,1,0:T(2,128)(2,1)} %reshape.189) | data formatting | bytes 8388608 | tf_op jit(solution)/shard_map/reshape | solution.py:95
  54.1 18.4 %all-to-all-start.2 = ((bf16[4,64,2,4096]{3,2,0,1:T(2,128)(2,1)}), bf16[4,64,2,4096]{3,2,0,1:T(2,128)(2,1)}, u32[]{:S(2)}, u32[]{:S(2)}) async-start(bf16[4,64,2,4096]{3,2,0,1:T(2,128)(2,1)} %copy.44), calls=%async_computation.3 | async-start | bytes 8388608 | tf_op jit(solution)/shard_map/all_to_all | solution.py:96
  72.6 5.5 collective-permute-start
  83.5 10.1 %all_gather.12 = s32[32,8]{1,0:T(8,128)S(1)} all-gather(s32[8,8]{1,0:T(8,128)S(1)} %copy-done.4), channel_id=1, replica_groups=mesh['expert'=64,'replica'=4] {'replica'}, dimensions={0}, use_global_device_ids=true | all-gather | bytes 1280 | tf_op jit(solution)/shard_map/all_gather | solution.py:82
  94.9 10.6 %all_gather.13 = bf16[32,4096]{1,0:T(8,128)(2,1)S(1)} all-gather(bf16[8,4096]{1,0:T(8,128)(2,1)S(1)} %get-tuple-element.14), channel_id=1, replica_groups=mesh['expert'=64,'replica'=4] {'replica'}, dimensions={0}, use_global_device_ids=true | all-gather | bytes 327680 | tf_op jit(solution)/shard_map/all_gather | solution.py:81
  108.9 7.8 %reshape.185 = bf16[4,64,2,4096]{3,2,1,0:T(2,128)(2,1)} reshape(bf16[4,128,4096]{2,1,0:T(8,128)(2,1)} %convolution_convert_fusion.3) | data formatting | bytes 8388608 | tf_op jit(solution)/shard_map/reshape | solution.py:95
  116.8 10.2 %copy.39 = bf16[4,64,2,4096]{3,2,0,1:T(2,128)(2,1)} copy(bf16[4,64,2,4096]{3,2,1,0:T(2,128)(2,1)} %reshape.185) | data formatting | bytes 8388608 | tf_op jit(solution)/shard_map/reshape | solution.py:95
  128.2 243.6 %collective-permute-done.3 = bf16[1,2,32]{2,1,0:T(2,128)(2,1)S(1)} collective-permute-done((bf16[1,2,32]{2,1,0:T(2,128)(2,1)S(1)}, bf16[1,2,32]{2,1,0:T(2,128)(2,1)S(1)}, u32[]{:S(2)}, u32[]{:S(2)}) %collective-permute-start.3) | collective-permute-done | bytes 160 | tf_op jit(solution)/shard_map/ppermute | solution.py:14
  373.0 5.4 mul.142
  378.5 11.5 %mul.143 = f32[2,4096,256]{2,1,0:T(8,128)} reshape(f32[2,32,128,2,128]{4,3,2,1,0:T(2,128)} %mul.142) | data formatting | bytes 16777216 | tf_op jit(solution)/shard_map/mul | solution.py:24
  390.0 5.4 mul.158
  395.5 11.5 %mul.159 = f32[2,4096,256]{2,1,0:T(8,128)} reshape(f32[2,32,128,2,128]{4,3,2,1,0:T(2,128)} %mul.158) | data formatting | bytes 16777216 | tf_op jit(solution)/shard_map/mul | solution.py:24
  409.9 10.6 %fusion = (bf16[2,4096,256]{2,1,0:T(8,128)(2,1)}, bf16[1,2,4096,256]{3,2,1,0:T(8,128)(2,1)}, bf16[2,4096,256]{2,1,0:T(8,128)(2,1)}) fusion(f32[2,4096,256]{2,1,0:T(8,128)} %mul.159, bf16[1,2,4096,256]{3,2,1,0:T(8,128)(2,1)} %collective-permute-done, bf16[1,2,4096,256]{3,2,1,0:T(8,128)(2,1)S(1)} %copy-done.2, pred[]{:T(512)S(6)} %eq.251, f32[2,4096,256]{2,1,0:T(8,128)} %mul.143), kind=kLoop, calls=%fused_computation.1 | loop fusion | flops 14680064 | bytes 37748736 | tf_op jit(solution)/shard_map/convert_element_type | solution.py:25
  420.5 75.5 %all-to-all-start = ((bf16[4,64,2,4096]{3,2,0,1:T(2,128)(2,1)}), bf16[4,64,2,4096]{3,2,0,1:T(2,128)(2,1)}, u32[]{:S(2)}, u32[]{:S(2)}) async-start(bf16[4,64,2,4096]{3,2,0,1:T(2,128)(2,1)} %copy.39), calls=%async_computation | async-start | bytes 8388608 | tf_op jit(solution)/shard_map/all_to_all | solution.py:96
  496.0 9.7 %copy.45 = bf16[4,64,2,4096]{3,2,1,0:T(2,128)(2,1)} copy(bf16[4,64,2,4096]{3,2,0,1:T(2,128)(2,1)} %all-to-all-done.2) | data formatting | bytes 8388608 | tf_op jit(solution)/shard_map/all_to_all | solution.py:96
  505.8 7.4 reshape.190
  519.8 11.9 %convolution_convert_fusion = bf16[512,4096]{1,0:T(8,128)(2,1)} fusion(f32[32,8,32,128]{3,2,1,0:T(8,128)} %bitcast.101, bf16[1,256,4096]{2,1,0:T(8,128)(2,1)} %broadcast_select_fusion.1, f32[512,256]{1,0:T(8,128)S(1)} %fusion.6, bf16[512,4096]{1,0:T(8,128)(2,1)} %reshape.190, bf16[2,4096,256]{2,1,0:T(8,128)(2,1)} %get-tuple-element.6), kind=kOutput, calls=%fused_computation.4 | convolution fusion | flops 2153512960 | bytes 17301504 | tf_op jit(solution)/shard_map/dot_general | solution.py:43
  531.7 7.6 %convert_element_type.200 = bf16[4,64,2,4096]{3,2,1,0:T(2,128)(2,1)} reshape(bf16[512,4096]{1,0:T(8,128)(2,1)} %convolution_convert_fusion) | data formatting | bytes 8388608 | tf_op jit(solution)/shard_map/convert_element_type | solution.py:67
  539.4 7.1 copy.47
  546.5 44.4 %all-to-all-done = bf16[4,64,2,4096]{3,2,0,1:T(2,128)(2,1)} async-done(((bf16[4,64,2,4096]{3,2,0,1:T(2,128)(2,1)}), bf16[4,64,2,4096]{3,2,0,1:T(2,128)(2,1)}, u32[]{:S(2)}, u32[]{:S(2)}) %all-to-all-start) | async-done | bytes 4194336 | tf_op jit(solution)/shard_map/all_to_all | solution.py:96
  590.9 9.7 %copy.40 = bf16[4,64,2,4096]{3,2,1,0:T(2,128)(2,1)} copy(bf16[4,64,2,4096]{3,2,0,1:T(2,128)(2,1)} %all-to-all-done) | data formatting | bytes 8388608 | tf_op jit(solution)/shard_map/all_to_all | solution.py:96
  600.6 7.4 %reshape.186 = bf16[512,4096]{1,0:T(8,128)(2,1)} reshape(bf16[4,64,2,4096]{3,2,1,0:T(2,128)(2,1)} %copy.40) | data formatting | bytes 8388608 | tf_op jit(solution)/shard_map/reshape | solution.py:98
  614.7 11.4 %convolution_convert_fusion.2 = bf16[512,4096]{1,0:T(8,128)(2,1)} fusion(f32[32,8,32,128]{3,2,1,0:T(8,128)} %bitcast.102, bf16[1,256,4096]{2,1,0:T(8,128)(2,1)S(1)} %copy-done.1, bf16[512,4096]{1,0:T(8,128)(2,1)} %reshape.186, bf16[2,4096,256]{2,1,0:T(8,128)(2,1)} %get-tuple-element.12, f32[512,256]{1,0:T(8,128)S(1)} %fusion.9), kind=kOutput, calls=%fused_computation.6 | convolution fusion | flops 2153512960 | bytes 17301504 | tf_op jit(solution)/shard_map/dot_general | solution.py:43
  626.1 7.7 %convert_element_type.179 = bf16[4,64,2,4096]{3,2,1,0:T(2,128)(2,1)} reshape(bf16[512,4096]{1,0:T(8,128)(2,1)} %convolution_convert_fusion.2) | data formatting | bytes 8388608 | tf_op jit(solution)/shard_map/convert_element_type | solution.py:67
  633.8 7.0 copy.42
  644.2 7.1 all-to-all-start.3
  651.3 35.9 %reduce-scatter.3.cloned.1.call-done = bf16[1,64,2,4096]{3,1,2,0:T(8,128)(2,1)} async-done(((bf16[4,64,2,4096]{3,1,2,0:T(8,128)(2,1)}), bf16[1,64,2,4096]{3,1,2,0:T(8,128)(2,1)}) %reduce-scatter.3.cloned.1.call-update) | async-done | bytes 1048592 | tf_op jit(solution)/shard_map/reduce_scatter | solution.py:66
  690.5 10.8 %all-to-all-start.1 = ((bf16[1,64,2,4096]{3,2,0,1:T(2,128)(2,1)}), bf16[1,64,2,4096]{3,2,0,1:T(2,128)(2,1)S(1)}, u32[]{:S(2)}, u32[]{:S(2)}) async-start(bf16[1,64,2,4096]{3,2,0,1:T(2,128)(2,1)} %copy.43), calls=%async_computation.2 | async-start | bytes 2097152 | tf_op jit(solution)/shard_map/all_to_all | solution.py:69
  704.9 24.4 %all-to-all-done.1 = bf16[1,64,2,4096]{3,2,0,1:T(2,128)(2,1)S(1)} async-done(((bf16[1,64,2,4096]{3,2,0,1:T(2,128)(2,1)}), bf16[1,64,2,4096]{3,2,0,1:T(2,128)(2,1)S(1)}, u32[]{:S(2)}, u32[]{:S(2)}) %all-to-all-start.1) | async-done | bytes 1048608 | tf_op jit(solution)/shard_map/all_to_all | solution.py:69
  (89 shorter events, 49.7 us)
Async XLA Ops:
  7.2 695.7 %copy-start = (f32[8,8]{1,0:T(8,128)S(1)}, f32[8,8]{1,0:T(8,128)}, u32[]{:S(2)}) copy-start(f32[8,8]{1,0:T(8,128)} %param.18) | copy-start | bytes 772
  54.1 23.9 %copy-start.1 = (bf16[1,256,4096]{2,1,0:T(8,128)(2,1)S(1)}, bf16[1,256,4096]{2,1,0:T(8,128)(2,1)}, u32[]{:S(2)}) copy-start(bf16[1,256,4096]{2,1,0:T(8,128)(2,1)} %param.24) | copy-start | bytes 6291460
  54.1 24.0 %copy-start.6 = (bf16[1,2,32,2]{2,3,1,0:T(2,128)(2,1)S(1)}, bf16[1,2,32,2]{2,3,1,0:T(2,128)(2,1)}, u32[]{:S(2)}) copy-start(bf16[1,2,32,2]{2,3,1,0:T(2,128)(2,1)} %param.23) | copy-start | bytes 772
  54.1 29.3 %copy-start.7 = (bf16[1,2,32]{2,1,0:T(2,128)(2,1)S(1)}, bf16[1,2,32]{2,1,0:T(2,128)(2,1)}, u32[]{:S(2)}) copy-start(bf16[1,2,32]{2,1,0:T(2,128)(2,1)} %param.25) | copy-start | bytes 388
  54.1 29.4 %copy-start.4 = (s32[8,8]{1,0:T(8,128)S(1)}, s32[8,8]{1,0:T(8,128)}, u32[]{:S(2)}) copy-start(s32[8,8]{1,0:T(8,128)} %param.15) | copy-start | bytes 772
  54.1 39.5 %copy-start.5 = (s32[64]{0:T(128)S(1)}, s32[64]{0:T(128)}, u32[]{:S(2)}) copy-start(s32[64]{0:T(128)} %param.20) | copy-start | bytes 772
  54.1 366.4 %all-to-all-start.2 = ((bf16[4,64,2,4096]{3,2,0,1:T(2,128)(2,1)}), bf16[4,64,2,4096]{3,2,0,1:T(2,128)(2,1)}, u32[]{:S(2)}, u32[]{:S(2)}) async-start(bf16[4,64,2,4096]{3,2,0,1:T(2,128)(2,1)} %copy.44), calls=%async_computation.3 | async-start | bytes 8388608 | tf_op jit(solution)/shard_map/all_to_all | solution.py:96
  72.6 336.1 %collective-permute-start = (bf16[1,2,4096,256]{3,2,1,0:T(8,128)(2,1)}, bf16[1,2,4096,256]{3,2,1,0:T(8,128)(2,1)}, u32[]{:S(2)}, u32[]{:S(2)}) collective-permute-start(bf16[1,2,4096,256]{3,2,1,0:T(8,128)(2,1)} %param.22), channel_id=1, source_target_pairs={{0,128},{128,0},{4,132},{132,4},{8,136},{136,8},{12,140},{140,12},... | collective-permute-start | bytes 12582920 | tf_op jit(solution)/shard_map/ppermute | solution.py:14
  78.0 329.0 %collective-permute-start.2 = (bf16[1,256,4096]{2,1,0:T(8,128)(2,1)S(1)}, bf16[1,256,4096]{2,1,0:T(8,128)(2,1)}, u32[]{:S(2)}, u32[]{:S(2)}) collective-permute-start(bf16[1,256,4096]{2,1,0:T(8,128)(2,1)S(1)} %copy-done.1), channel_id=1, source_target_pairs={{0,128},{128,0},{4,132},{132,4},{8,136},{136,8},{12,140},{140,12},... | collective-permute-start | bytes 6291464 | tf_op jit(solution)/shard_map/ppermute | solution.py:14
  78.2 294.2 %collective-permute-start.1 = (bf16[1,2,32,2]{2,3,1,0:T(2,128)(2,1)S(1)}, bf16[1,2,32,2]{2,3,1,0:T(2,128)(2,1)S(1)}, u32[]{:S(2)}, u32[]{:S(2)}) collective-permute-start(bf16[1,2,32,2]{2,3,1,0:T(2,128)(2,1)S(1)} %copy-done.6), channel_id=1, source_target_pairs={{0,128},{128,0},{4,132},{132,4},{8,136},{136,8},{12,140},{140,12},... | collective-permute-start | bytes 776 | tf_op jit(solution)/shard_map/ppermute | solution.py:14
  83.4 288.4 %collective-permute-start.3 = (bf16[1,2,32]{2,1,0:T(2,128)(2,1)S(1)}, bf16[1,2,32]{2,1,0:T(2,128)(2,1)S(1)}, u32[]{:S(2)}, u32[]{:S(2)}) collective-permute-start(bf16[1,2,32]{2,1,0:T(2,128)(2,1)S(1)} %copy-done.7), channel_id=1, source_target_pairs={{0,128},{128,0},{4,132},{132,4},{8,136},{136,8},{12,140},{140,12},... | collective-permute-start | bytes 392 | tf_op jit(solution)/shard_map/ppermute | solution.py:14
  116.8 10.2 %copy-start.9 = (s32[64]{0:T(128)S(1)}, s32[64]{0:T(128)}, u32[]{:S(2)}) copy-start(s32[64]{0:T(128)} %param.21) | copy-start | bytes 772
  407.0 2.9 copy-start.2
  420.5 170.4 %all-to-all-start = ((bf16[4,64,2,4096]{3,2,0,1:T(2,128)(2,1)}), bf16[4,64,2,4096]{3,2,0,1:T(2,128)(2,1)}, u32[]{:S(2)}, u32[]{:S(2)}) async-start(bf16[4,64,2,4096]{3,2,0,1:T(2,128)(2,1)} %copy.39), calls=%async_computation | async-start | bytes 8388608 | tf_op jit(solution)/shard_map/all_to_all | solution.py:96
  496.0 144.9 %reduce-scatter.5.cloned.1.call-start = ((), (), s32[]{:S(2)}) async-start(), calls=%async_computation.7 | async-start | bytes 5242880 | tf_op jit(solution)/shard_map/reduce_scatter | solution.py:66
  546.4 140.7 %reduce-scatter.3.cloned.1.call-start = ((), (), s32[]{:S(2)}) async-start(), calls=%async_computation.6 | async-start | bytes 5242880 | tf_op jit(solution)/shard_map/reduce_scatter | solution.py:66
  640.8 60.4 %copy-start.3 = (s32[8,8]{1,0:T(8,128)S(1)}, s32[8,8]{1,0:T(8,128)}, u32[]{:S(2)}) copy-start(s32[8,8]{1,0:T(8,128)} %param.16) | copy-start | bytes 772
  640.8 62.3 %copy-start.8 = (f32[8,8]{1,0:T(8,128)S(1)}, f32[8,8]{1,0:T(8,128)}, u32[]{:S(2)}) copy-start(f32[8,8]{1,0:T(8,128)} %param.17) | copy-start | bytes 772
  644.2 46.3 %all-to-all-start.3 = ((bf16[1,64,2,4096]{3,2,0,1:T(2,128)(2,1)}), bf16[1,64,2,4096]{3,2,0,1:T(2,128)(2,1)S(1)}, u32[]{:S(2)}, u32[]{:S(2)}) async-start(bf16[1,64,2,4096]{3,2,0,1:T(2,128)(2,1)} %copy.48), calls=%async_computation.5 | async-start | bytes 2097152 | tf_op jit(solution)/shard_map/all_to_all | solution.py:69
  690.5 38.9 %all-to-all-start.1 = ((bf16[1,64,2,4096]{3,2,0,1:T(2,128)(2,1)}), bf16[1,64,2,4096]{3,2,0,1:T(2,128)(2,1)S(1)}, u32[]{:S(2)}, u32[]{:S(2)}) async-start(bf16[1,64,2,4096]{3,2,0,1:T(2,128)(2,1)} %copy.43), calls=%async_computation.2 | async-start | bytes 2097152 | tf_op jit(solution)/shard_map/all_to_all | solution.py:69
Sparse Core Ops, SparseCore 0:
  546.6 49.7 reduce-scatter.4
  640.9 46.1 reduce-scatter.2
where the time goes:
time: 749 us; the launch traced here: 738 us
  waiting for transfers between devices  348 us (46%)
  local copies, waits for them, and re-layouts  148 us (20%)
  starting transfers between devices  123 us (16%)
  matrix products  40.9 us (5%)
  blocking collectives  40.4 us (5%)
  other arithmetic  22.3 us (3%)
  between operations  15.4 us (2%)
    ppermute x4, waiting for transfers between devices, partner(): return lax.ppermute(block, axis, route)  244 us
    all_to_all x2, starting transfers between devices, decode_step(): lax.all_to_all(outgoing, 'expert', split_axis=1, concat_axis=1, tiled=True)  93.9 us
    all_to_all x2, waiting for transfers between devices, decode_step(): lax.all_to_all(outgoing, 'expert', split_axis=1, concat_axis=1, tiled=True)  44.4 us
    mul x6, local copies, waits for them, and re-layouts, dequantize(): scaled = blocked * scales.astype(jnp.float32)[..., :, None, :, None]  39 us
    reduce_scatter x2, waiting for transfers between devices, finish(): lax.psum_scatter(partial_terms.astype(jnp.bfloat16), 'replica', scatter_d...  35.9 us
    reshape x4, local copies, waits for them, and re-layouts, decode_step(): outgoing.astype(jnp.bfloat16).reshape(copies, experts, capacity, features)  35.8 us
    convert_element_type x4, local copies, waits for them, and re-layouts, finish(): partial_terms.astype(jnp.bfloat16)  29.4 us
    all_to_all x2, waiting for transfers between devices, finish(): lax.all_to_all(summed, 'expert', split_axis=1, concat_axis=1, tiled=True)  24.4 us
  transfers between devices with their start and end apart: 10, of which 4 were waited for; matrix products, arithmetic and copies ran while one was open for 25% of the time, Pallas kernels for 0%

commit v1 on v0

--- a/solution.py
+++ b/solution.py
@@ -66,7 +66,12 @@
     summed = lax.psum_scatter(
         partial_terms.astype(jnp.bfloat16), "replica", scatter_dimension=0, tiled=True
     )
-    return lax.all_to_all(summed, "expert", split_axis=1, concat_axis=1, tiled=True)
+    return jnp.concatenate(
+        lax.all_to_all(
+            jnp.stack(jnp.split(summed, lax.axis_size("expert"), axis=1)), "expert", 0, 0
+        ),
+        axis=1,
+    )
 
 
 def decode_step(hidden, routes, mixing, norm_gain, owner_slots, weights):

time: 749 us -> 803 us (1.072)
  local copies, waits for them, and re-layouts: 148 us -> 238 us
  waiting for transfers between devices: 348 us -> 312 us
    unnamed x20 -> x150, local copies, waits for them, and re-layouts: 1.32 us -> 80.2 us
    reduce_scatter x2, waiting for transfers between devices: 35.9 us -> 0.04 us  [finish(): lax.psum_scatter(partial_terms.astype(jnp.bfloat16), 'replica', scatter_d...]
    split x0 -> x8, local copies, waits for them, and re-layouts: none -> 16.6 us  [finish(): jnp.split(summed, lax.axis_size('expert'), axis=1)]
  transfers between devices with their start and end apart: 10 -> 10, of which waited for: 4 -> 3; matrix products, arithmetic and copies ran while one was open for 25% -> 34% of each run, Pallas kernels for 0% -> 0%
where the time goes in v1:
time: 803 us; the launch traced here: 792 us
  waiting for transfers between devices  312 us (39%)
  local copies, waits for them, and re-layouts  238 us (30%)
  starting transfers between devices  123 us (15%)
  matrix products  40.9 us (5%)
  blocking collectives  40.4 us (5%)
  other arithmetic  22.3 us (3%)
  between operations  15.6 us (2%)
    ppermute x4, waiting for transfers between devices, partner(): return lax.ppermute(block, axis, route)  244 us
    all_to_all x2, starting transfers between devices, decode_step(): lax.all_to_all(outgoing, 'expert', split_axis=1, concat_axis=1, tiled=True)  93.9 us
    unnamed x150, local copies, waits for them, and re-layouts  80.2 us
    all_to_all x2, waiting for transfers between devices, decode_step(): lax.all_to_all(outgoing, 'expert', split_axis=1, concat_axis=1, tiled=True)  44.2 us
    mul x6, local copies, waits for them, and re-layouts, dequantize(): scaled = blocked * scales.astype(jnp.float32)[..., :, None, :, None]  39 us
    reshape x4, local copies, waits for them, and re-layouts, decode_step(): outgoing.astype(jnp.bfloat16).reshape(copies, experts, capacity, features)  35.8 us
    convert_element_type x4, local copies, waits for them, and re-layouts, finish(): partial_terms.astype(jnp.bfloat16)  29.6 us
    all_to_all x2, waiting for transfers between devices, finish(): lax.all_to_all(jnp.stack(jnp.split(summed, lax.axis_size('expert'), axis=...  24.4 us
  transfers between devices with their start and end apart: 10, of which 3 were waited for; matrix products, arithmetic and copies ran while one was open for 34% of the time, Pallas kernels for 0%

profile of v1, /device:TPU:1, one launch (start us, length us, event | category | flops | bytes accessed | tf_op | source)
XLA Modules:
  0.0 792.4 jit_solution(9742034736337061482)
XLA Ops:
  8.7 10.4 %all_gather.14 = s32[32,8]{1,0:T(8,128)S(1)} all-gather(s32[8,8]{1,0:T(8,128)} %param.16), channel_id=1, replica_groups=mesh['expert'=64,'replica'=4] {'replica'}, dimensions={0}, use_global_device_ids=true | all-gather | bytes 1280 | tf_op jit(solution)/shard_map/all_gather | solution.py:87
  23.6 9.4 %all_gather.15 = bf16[32,4096]{1,0:T(8,128)(2,1)S(1)} all-gather(bf16[8,4096]{1,0:T(8,128)(2,1)S(1)} %get-tuple-element.141), channel_id=1, replica_groups=mesh['expert'=64,'replica'=4] {'replica'}, dimensions={0}, use_global_device_ids=true | all-gather | bytes 327680 | tf_op jit(solution)/shard_map/all_gather | solution.py:86
  36.3 7.6 reshape.182
  43.9 10.2 %copy.354 = bf16[4,64,2,4096]{3,2,0,1:T(2,128)(2,1)} copy(bf16[4,64,2,4096]{3,2,1,0:T(2,128)(2,1)} %reshape.182) | data formatting | bytes 8388608 | tf_op jit(solution)/shard_map/reshape | solution.py:100
  54.1 18.4 %all-to-all-start.2 = ((bf16[4,64,2,4096]{3,2,0,1:T(2,128)(2,1)}), bf16[4,64,2,4096]{3,2,0,1:T(2,128)(2,1)}, u32[]{:S(2)}, u32[]{:S(2)}) async-start(bf16[4,64,2,4096]{3,2,0,1:T(2,128)(2,1)} %copy.354), calls=%async_computation.3 | async-start | bytes 8388608 | tf_op jit(solution)/shard_map/all_to_all | solution.py:101
  72.6 5.5 collective-permute-start
  78.2 5.3 collective-permute-start.1
  83.5 10.1 %all_gather.12 = s32[32,8]{1,0:T(8,128)S(1)} all-gather(s32[8,8]{1,0:T(8,128)S(1)} %copy-done.6), channel_id=1, replica_groups=mesh['expert'=64,'replica'=4] {'replica'}, dimensions={0}, use_global_device_ids=true | all-gather | bytes 1280 | tf_op jit(solution)/shard_map/all_gather | solution.py:87
  94.9 10.6 %all_gather.13 = bf16[32,4096]{1,0:T(8,128)(2,1)S(1)} all-gather(bf16[8,4096]{1,0:T(8,128)(2,1)S(1)} %get-tuple-element.142), channel_id=1, replica_groups=mesh['expert'=64,'replica'=4] {'replica'}, dimensions={0}, use_global_device_ids=true | all-gather | bytes 327680 | tf_op jit(solution)/shard_map/all_gather | solution.py:86
  108.9 7.8 reshape.179
  116.8 10.2 %copy.287 = bf16[4,64,2,4096]{3,2,0,1:T(2,128)(2,1)} copy(bf16[4,64,2,4096]{3,2,1,0:T(2,128)(2,1)} %reshape.179) | data formatting | bytes 8388608 | tf_op jit(solution)/shard_map/reshape | solution.py:100
  128.2 243.6 %collective-permute-done.3 = bf16[1,2,32]{2,1,0:T(2,128)(2,1)S(1)} collective-permute-done((bf16[1,2,32]{2,1,0:T(2,128)(2,1)S(1)}, bf16[1,2,32]{2,1,0:T(2,128)(2,1)S(1)}, u32[]{:S(2)}, u32[]{:S(2)}) %collective-permute-start.3) | collective-permute-done | bytes 160 | tf_op jit(solution)/shard_map/ppermute | solution.py:14
  373.0 5.4 mul.142
  378.5 11.5 %mul.143 = f32[2,4096,256]{2,1,0:T(8,128)} reshape(f32[2,32,128,2,128]{4,3,2,1,0:T(2,128)} %mul.142) | data formatting | bytes 16777216 | tf_op jit(solution)/shard_map/mul | solution.py:24
  390.0 5.4 mul.158
  395.5 11.5 %mul.159 = f32[2,4096,256]{2,1,0:T(8,128)} reshape(f32[2,32,128,2,128]{4,3,2,1,0:T(2,128)} %mul.158) | data formatting | bytes 16777216 | tf_op jit(solution)/shard_map/mul | solution.py:24
  409.9 10.6 %fusion = (bf16[2,4096,256]{2,1,0:T(8,128)(2,1)}, bf16[1,2,4096,256]{3,2,1,0:T(8,128)(2,1)}, bf16[2,4096,256]{2,1,0:T(8,128)(2,1)}) fusion(f32[2,4096,256]{2,1,0:T(8,128)} %mul.159, bf16[1,2,4096,256]{3,2,1,0:T(8,128)(2,1)} %collective-permute-done, bf16[1,2,4096,256]{3,2,1,0:T(8,128)(2,1)S(1)} %copy-done.2, pred[]{:T(512)S(6)} %eq.251, f32[2,4096,256]{2,1,0:T(8,128)} %mul.143), kind=kLoop, calls=%fused_computation.1 | loop fusion | flops 14680064 | bytes 37748736 | tf_op jit(solution)/shard_map/convert_element_type | solution.py:25
  420.5 75.5 %all-to-all-start = ((bf16[4,64,2,4096]{3,2,0,1:T(2,128)(2,1)}), bf16[4,64,2,4096]{3,2,0,1:T(2,128)(2,1)}, u32[]{:S(2)}, u32[]{:S(2)}) async-start(bf16[4,64,2,4096]{3,2,0,1:T(2,128)(2,1)} %copy.287), calls=%async_computation | async-start | bytes 8388608 | tf_op jit(solution)/shard_map/all_to_all | solution.py:101
  496.0 9.7 %copy.355 = bf16[4,64,2,4096]{3,2,1,0:T(2,128)(2,1)} copy(bf16[4,64,2,4096]{3,2,0,1:T(2,128)(2,1)} %all-to-all-done.2) | data formatting | bytes 8388608 | tf_op jit(solution)/shard_map/all_to_all | solution.py:101
  505.8 7.4 reshape.183
  519.8 11.9 %convolution_convert_fusion = bf16[512,4096]{1,0:T(8,128)(2,1)} fusion(f32[32,8,32,128]{3,2,1,0:T(8,128)} %bitcast.605, bf16[1,256,4096]{2,1,0:T(8,128)(2,1)} %broadcast_select_fusion.1, f32[512,256]{1,0:T(8,128)S(1)} %fusion.6, bf16[512,4096]{1,0:T(8,128)(2,1)} %reshape.183, bf16[2,4096,256]{2,1,0:T(8,128)(2,1)} %get-tuple-element.6), kind=kOutput, calls=%fused_computation.4 | convolution fusion | flops 2153512960 | bytes 17301504 | tf_op jit(solution)/shard_map/dot_general | solution.py:43
  531.7 7.6 convert_element_type.200
  539.4 7.1 copy.357
  546.7 44.2 %all-to-all-done = bf16[4,64,2,4096]{3,2,0,1:T(2,128)(2,1)} async-done(((bf16[4,64,2,4096]{3,2,0,1:T(2,128)(2,1)}), bf16[4,64,2,4096]{3,2,0,1:T(2,128)(2,1)}, u32[]{:S(2)}, u32[]{:S(2)}) %all-to-all-start) | async-done | bytes 4194336 | tf_op jit(solution)/shard_map/all_to_all | solution.py:101
  590.9 9.7 %copy.288 = bf16[4,64,2,4096]{3,2,1,0:T(2,128)(2,1)} copy(bf16[4,64,2,4096]{3,2,0,1:T(2,128)(2,1)} %all-to-all-done) | data formatting | bytes 8388608 | tf_op jit(solution)/shard_map/all_to_all | solution.py:101
  600.6 7.2 reshape.180
  614.5 11.4 %convolution_convert_fusion.2 = bf16[512,4096]{1,0:T(8,128)(2,1)} fusion(f32[32,8,32,128]{3,2,1,0:T(8,128)} %bitcast.606, bf16[1,256,4096]{2,1,0:T(8,128)(2,1)S(1)} %copy-done.1, bf16[512,4096]{1,0:T(8,128)(2,1)} %reshape.180, bf16[2,4096,256]{2,1,0:T(8,128)(2,1)} %get-tuple-element.12, f32[512,256]{1,0:T(8,128)S(1)} %fusion.9), kind=kOutput, calls=%fused_computation.6 | convolution fusion | flops 2153512960 | bytes 17301504 | tf_op jit(solution)/shard_map/dot_general | solution.py:43
  625.9 7.9 convert_element_type.179
  633.8 7.0 copy.290
  689.5 7.2 all-to-all-start.3
  745.0 10.3 %all-to-all-start.1 = ((bf16[64,1,1,2,4096]{4,3,2,1,0:T(2,128)(2,1)}), bf16[64,1,1,2,4096]{4,3,2,1,0:T(2,128)(2,1)S(1)}, u32[]{:S(2)}, u32[]{:S(2)}) async-start(bf16[64,1,1,2,4096]{4,3,2,1,0:T(2,128)(2,1)} %constant_dynamic-update-slice_fusion), calls=%async_computation.2 | async-start | bytes 2097152 | tf_op jit(solution)/shard_map/all_to_all | solution.py:70
  759.1 24.4 %all-to-all-done.1 = bf16[64,1,1,2,4096]{4,3,2,1,0:T(2,128)(2,1)S(1)} async-done(((bf16[64,1,1,2,4096]{4,3,2,1,0:T(2,128)(2,1)}), bf16[64,1,1,2,4096]{4,3,2,1,0:T(2,128)(2,1)S(1)}, u32[]{:S(2)}, u32[]{:S(2)}) %all-to-all-start.1) | async-done | bytes 1048608 | tf_op jit(solution)/shard_map/all_to_all | solution.py:70
  (227 shorter events, 134.7 us)
Async XLA Ops:
  7.2 749.8 %copy-start = (f32[8,8]{1,0:T(8,128)S(1)}, f32[8,8]{1,0:T(8,128)}, u32[]{:S(2)}) copy-start(f32[8,8]{1,0:T(8,128)} %param.18) | copy-start | bytes 772
  54.1 23.9 %copy-start.1 = (bf16[1,256,4096]{2,1,0:T(8,128)(2,1)S(1)}, bf16[1,256,4096]{2,1,0:T(8,128)(2,1)}, u32[]{:S(2)}) copy-start(bf16[1,256,4096]{2,1,0:T(8,128)(2,1)} %param.24) | copy-start | bytes 6291460
  54.1 24.0 %copy-start.8 = (bf16[1,2,32,2]{2,3,1,0:T(2,128)(2,1)S(1)}, bf16[1,2,32,2]{2,3,1,0:T(2,128)(2,1)}, u32[]{:S(2)}) copy-start(bf16[1,2,32,2]{2,3,1,0:T(2,128)(2,1)} %param.23) | copy-start | bytes 772
  54.1 29.3 %copy-start.9 = (bf16[1,2,32]{2,1,0:T(2,128)(2,1)S(1)}, bf16[1,2,32]{2,1,0:T(2,128)(2,1)}, u32[]{:S(2)}) copy-start(bf16[1,2,32]{2,1,0:T(2,128)(2,1)} %param.25) | copy-start | bytes 388
  54.1 29.4 %copy-start.6 = (s32[8,8]{1,0:T(8,128)S(1)}, s32[8,8]{1,0:T(8,128)}, u32[]{:S(2)}) copy-start(s32[8,8]{1,0:T(8,128)} %param.15) | copy-start | bytes 772
  54.1 39.5 %copy-start.7 = (s32[64]{0:T(128)S(1)}, s32[64]{0:T(128)}, u32[]{:S(2)}) copy-start(s32[64]{0:T(128)} %param.20) | copy-start | bytes 772
  54.1 366.4 %all-to-all-start.2 = ((bf16[4,64,2,4096]{3,2,0,1:T(2,128)(2,1)}), bf16[4,64,2,4096]{3,2,0,1:T(2,128)(2,1)}, u32[]{:S(2)}, u32[]{:S(2)}) async-start(bf16[4,64,2,4096]{3,2,0,1:T(2,128)(2,1)} %copy.354), calls=%async_computation.3 | async-start | bytes 8388608 | tf_op jit(solution)/shard_map/all_to_all | solution.py:101
  72.6 336.1 %collective-permute-start = (bf16[1,2,4096,256]{3,2,1,0:T(8,128)(2,1)}, bf16[1,2,4096,256]{3,2,1,0:T(8,128)(2,1)}, u32[]{:S(2)}, u32[]{:S(2)}) collective-permute-start(bf16[1,2,4096,256]{3,2,1,0:T(8,128)(2,1)} %param.22), channel_id=1, source_target_pairs={{0,128},{128,0},{4,132},{132,4},{8,136},{136,8},{12,140},{140,12},... | collective-permute-start | bytes 12582920 | tf_op jit(solution)/shard_map/ppermute | solution.py:14
  78.0 329.0 %collective-permute-start.2 = (bf16[1,256,4096]{2,1,0:T(8,128)(2,1)S(1)}, bf16[1,256,4096]{2,1,0:T(8,128)(2,1)}, u32[]{:S(2)}, u32[]{:S(2)}) collective-permute-start(bf16[1,256,4096]{2,1,0:T(8,128)(2,1)S(1)} %copy-done.1), channel_id=1, source_target_pairs={{0,128},{128,0},{4,132},{132,4},{8,136},{136,8},{12,140},{140,12},... | collective-permute-start | bytes 6291464 | tf_op jit(solution)/shard_map/ppermute | solution.py:14
  78.2 294.2 %collective-permute-start.1 = (bf16[1,2,32,2]{2,3,1,0:T(2,128)(2,1)S(1)}, bf16[1,2,32,2]{2,3,1,0:T(2,128)(2,1)S(1)}, u32[]{:S(2)}, u32[]{:S(2)}) collective-permute-start(bf16[1,2,32,2]{2,3,1,0:T(2,128)(2,1)S(1)} %copy-done.8), channel_id=1, source_target_pairs={{0,128},{128,0},{4,132},{132,4},{8,136},{136,8},{12,140},{140,12},... | collective-permute-start | bytes 776 | tf_op jit(solution)/shard_map/ppermute | solution.py:14
  83.4 288.4 %collective-permute-start.3 = (bf16[1,2,32]{2,1,0:T(2,128)(2,1)S(1)}, bf16[1,2,32]{2,1,0:T(2,128)(2,1)S(1)}, u32[]{:S(2)}, u32[]{:S(2)}) collective-permute-start(bf16[1,2,32]{2,1,0:T(2,128)(2,1)S(1)} %copy-done.9), channel_id=1, source_target_pairs={{0,128},{128,0},{4,132},{132,4},{8,136},{136,8},{12,140},{140,12},... | collective-permute-start | bytes 392 | tf_op jit(solution)/shard_map/ppermute | solution.py:14
  116.8 10.2 %copy-start.11 = (s32[64]{0:T(128)S(1)}, s32[64]{0:T(128)}, u32[]{:S(2)}) copy-start(s32[64]{0:T(128)} %param.21) | copy-start | bytes 772
  407.0 2.9 copy-start.2
  420.5 170.4 %all-to-all-start = ((bf16[4,64,2,4096]{3,2,0,1:T(2,128)(2,1)}), bf16[4,64,2,4096]{3,2,0,1:T(2,128)(2,1)}, u32[]{:S(2)}, u32[]{:S(2)}) async-start(bf16[4,64,2,4096]{3,2,0,1:T(2,128)(2,1)} %copy.287), calls=%async_computation | async-start | bytes 8388608 | tf_op jit(solution)/shard_map/all_to_all | solution.py:101
  496.0 144.9 %reduce-scatter.5.cloned.1.call-start = ((), (), s32[]{:S(2)}) async-start(), calls=%async_computation.7 | async-start | bytes 5242880 | tf_op jit(solution)/shard_map/reduce_scatter | solution.py:66
  546.4 150.3 %reduce-scatter.3.cloned.1.call-start = ((), (), s32[]{:S(2)}) async-start(), calls=%async_computation.6 | async-start | bytes 5242880 | tf_op jit(solution)/shard_map/reduce_scatter | solution.py:66
  640.9 35.4 %copy-start.4 = (bf16[1,64,2,4096]{3,1,2,0:T(8,128)(2,1)S(1)}, bf16[1,64,2,4096]{3,1,2,0:T(8,128)(2,1)}, u32[]{:S(2)}) copy-start(bf16[1,64,2,4096]{3,1,2,0:T(8,128)(2,1)} %reduce-scatter.5.cloned.1.call-done) | copy-start | bytes 3145732
  689.5 55.5 %all-to-all-start.3 = ((bf16[64,1,1,2,4096]{4,3,2,1,0:T(2,128)(2,1)}), bf16[64,1,1,2,4096]{4,3,2,1,0:T(2,128)(2,1)S(1)}, u32[]{:S(2)}, u32[]{:S(2)}) async-start(bf16[64,1,1,2,4096]{4,3,2,1,0:T(2,128)(2,1)} %constant_dynamic-update-slice_fusion.64), calls=%async_computation.5 | async-start | bytes 2097152 | tf_op jit(solution)/shard_map/all_to_all | solution.py:70
  696.8 35.0 %copy-start.3 = (bf16[1,64,2,4096]{3,1,2,0:T(8,128)(2,1)S(1)}, bf16[1,64,2,4096]{3,1,2,0:T(8,128)(2,1)}, u32[]{:S(2)}) copy-start(bf16[1,64,2,4096]{3,1,2,0:T(8,128)(2,1)} %reduce-scatter.3.cloned.1.call-done) | copy-start | bytes 3145732
  702.9 52.5 %copy-start.5 = (s32[8,8]{1,0:T(8,128)S(1)}, s32[8,8]{1,0:T(8,128)}, u32[]{:S(2)}) copy-start(s32[8,8]{1,0:T(8,128)} %param.16) | copy-start | bytes 772
  705.8 51.4 %copy-start.10 = (f32[8,8]{1,0:T(8,128)S(1)}, f32[8,8]{1,0:T(8,128)}, u32[]{:S(2)}) copy-start(f32[8,8]{1,0:T(8,128)} %param.17) | copy-start | bytes 772
  745.0 38.5 %all-to-all-start.1 = ((bf16[64,1,1,2,4096]{4,3,2,1,0:T(2,128)(2,1)}), bf16[64,1,1,2,4096]{4,3,2,1,0:T(2,128)(2,1)S(1)}, u32[]{:S(2)}, u32[]{:S(2)}) async-start(bf16[64,1,1,2,4096]{4,3,2,1,0:T(2,128)(2,1)} %constant_dynamic-update-slice_fusion), calls=%async_computation.2 | async-start | bytes 2097152 | tf_op jit(solution)/shard_map/all_to_all | solution.py:70
Sparse Core Ops, SparseCore 0:
  546.6 49.7 reduce-scatter.4
  641.0 46.1 reduce-scatter.2
